TPU v7x, 32 devices: a whole 2x2x4 slice. The times are simulated.
32 devices in a mesh: gx: 4 (over x, core), gy: 8 (over z, y).
Axes of the slice: x: 2, y: 2, z: 4, core: 2. Of those that a mesh axis runs over, the one named last changes fastest.
Arguments:
- patches: bfloat16 [4096, 1664], P('gy', 'gx'), may hold values from -6 to 6
- segment_ids: int32 [4096], P('gy'), may hold values from 0 to 31, as said below
- image_requests: int32 [32], replicated, may hold values from 0 to 7
- merge_index: int32 [1024, 4], P('gy'), may hold values from 0 to 4095, as said below
- qkv_weight: bfloat16 [1664, 3, 1664], P('gy', None, 'gx'), may hold values from -128 to 128
- out_weight: bfloat16 [1664, 1664], P('gx', 'gy'), may hold values from -0.15625 to 0.15625
- up_weight: bfloat16 [1664, 8192], P('gy', 'gx'), may hold values from -0.15625 to 0.15625
- down_weight: bfloat16 [8192, 1664], P('gx', 'gy'), may hold values from -0.0625 to 0.0625
- merge_weight: bfloat16 [6656, 4096], P('gy', 'gx'), may hold values from -0.078125 to 0.078125
Outputs:
- merged: bfloat16 [1024, 4096], P('gy', 'gx')
- request_norms: float32 [8], replicated
- top_logit: float32 [], replicated
Inputs may be any that keep to these rules, and one draw needn't show every extreme that they name: `segment_ids`: segment ids never fall along the tokens; the 512 tokens of block b (tokens b * 512 onward) hold exactly the images b * 4 to (b + 1) * 4 - 1, each a multiple of 4 tokens long. `merge_index`: every token stands in exactly one merged row; the four tokens of merged row m belong to one image, in the block of 512 tokens that holds token 4 * m.
All inputs are finite; a program needn't handle non-finite values.
Results may differ from a plain program's by a relative error of at most 0.011.
Values may be sent and summed in bfloat16 or wider, within the bound.
A program may use at most 128 MiB of HBM per device.

v0:
```python
import math
import jax
import jax.numpy as jnp
from jax import lax
from jax.sharding import PartitionSpec as P

HEAD = 104
IMG_GRP = 4


def layer_norm(values):
    center = jnp.mean(values, axis=-1, keepdims=True)
    square = jnp.mean(values * values, axis=-1, keepdims=True)
    return (values - center) * lax.rsqrt(square - center * center + 1e-06)


def add_columns(left, piece):
    flat = piece.reshape(piece.shape[0], -1)
    return jnp.dot(left, flat, preferred_element_type=jnp.float32)


def finish_sum(head_partial, stream_full, feat_share):
    own_index = lax.axis_index("gx")
    summed = lax.psum(head_partial, "gx")
    new_full = (stream_full.astype(jnp.float32) + summed).astype(jnp.bfloat16)
    new_share = lax.dynamic_slice_in_dim(new_full, own_index * feat_share, feat_share, 1)
    return (new_full, new_share)


def per_device(
    patches,
    segment_ids,
    image_requests,
    merge_index,
    qkv_weight,
    out_weight,
    up_weight,
    down_weight,
    merge_weight,
):
    tok_rows = patches.shape[0]
    feat_share = patches.shape[1]
    group_index = lax.axis_index("gy")
    stream_full = lax.all_gather(patches, "gx", axis=1, tiled=True)
    normed = layer_norm(stream_full.astype(jnp.float32)).astype(jnp.bfloat16)
    head_share = qkv_weight.shape[2]
    local_heads = head_share // HEAD
    projected = add_columns(normed, lax.all_gather(qkv_weight, "gy", axis=0, tiled=True))
    projected = projected.astype(jnp.bfloat16).reshape(tok_rows, 3, local_heads, HEAD)
    scores = jnp.einsum(
        "qhe,khe->hqk", projected[:, 0], projected[:, 1], preferred_element_type=jnp.float32
    ) / math.sqrt(HEAD)
    allowed = segment_ids[:, None] == segment_ids[None, :]
    scores = jnp.where(allowed[None], scores, -1e30)
    probs = jax.nn.softmax(scores, axis=-1).astype(jnp.bfloat16)
    mixed = jnp.einsum("hqk,khe->qhe", probs, projected[:, 2], preferred_element_type=jnp.float32)
    mixed = mixed.astype(jnp.bfloat16).reshape(tok_rows, head_share)
    head_partial = jnp.dot(
        mixed,
        lax.all_gather(out_weight, "gy", axis=1, tiled=True),
        preferred_element_type=jnp.float32,
    )
    stream_full, stream_share = finish_sum(head_partial, stream_full, feat_share)
    normed_two = layer_norm(stream_full.astype(jnp.float32)).astype(jnp.bfloat16)
    hidden = add_columns(normed_two, lax.all_gather(up_weight, "gy", axis=0, tiled=True))
    hidden = jax.nn.gelu(hidden, approximate=False).astype(jnp.bfloat16)
    unit_partial = jnp.dot(
        hidden,
        lax.all_gather(down_weight, "gy", axis=1, tiled=True),
        preferred_element_type=jnp.float32,
    )
    final_full, final_share = finish_sum(unit_partial, stream_full, feat_share)
    row_squares = jnp.sum(jnp.square(final_share.astype(jnp.float32)), axis=1)
    image_ids = group_index * IMG_GRP + jnp.arange(IMG_GRP, dtype=jnp.int32)
    member = segment_ids[:, None] == image_ids[None, :]
    image_sq = jnp.sum(jnp.where(member, row_squares[:, None], 0.0), axis=0)
    local_requests = lax.dynamic_slice_in_dim(image_requests, group_index * IMG_GRP, IMG_GRP)
    request_count = image_requests.shape[0] // 4
    owner = local_requests[:, None] == jnp.arange(request_count, dtype=jnp.int32)[None, :]
    request_part = jnp.sum(jnp.where(owner, image_sq[:, None], 0.0), axis=0)
    local_index = (merge_index - group_index * tok_rows).reshape(-1)
    joined = jnp.take(final_full, local_index, axis=0).reshape(
        merge_index.shape[0], 4 * final_full.shape[1]
    )
    logits = add_columns(joined, lax.all_gather(merge_weight, "gy", axis=0, tiled=True))
    local_top = jnp.max(logits)
    request_sq = lax.psum(request_part, ("gx", "gy"))
    top_logit = lax.pmax(local_top, ("gx", "gy"))
    return (logits.astype(jnp.bfloat16), jnp.sqrt(request_sq), top_logit)


def solution(mesh):
    in_specs = (
        P("gy", "gx"),
        P("gy"),
        P(),
        P("gy", None),
        P("gy", None, "gx"),
        P("gx", "gy"),
        P("gy", "gx"),
        P("gx", "gy"),
        P("gy", "gx"),
    )
    out_specs = (P("gy", "gx"), P(), P())
    return jax.shard_map(
        per_device, mesh=mesh, in_specs=in_specs, out_specs=out_specs, check_vma=False
    )
```

profile of v0, /device:TPU:0, one launch (start us, length us, event | category | flops | bytes accessed | tf_op | source)
XLA Modules:
  0.0 815.3 jit_solution(6109742581719975203)
XLA Ops:
  7.9 2.6 copy.29
  10.6 1.7 copy.32
  13.4 19.3 %all-gather.7.cloned.1.call-done = bf16[512,1664]{0,1:T(8,128)(2,1)} async-done(((bf16[512,416]{0,1:T(8,128)(2,1)}), bf16[512,1664]{0,1:T(8,128)(2,1)}) %all-gather.7.cloned.1.call-update) | async-done | bytes 1703952 | tf_op jit(solution)/shard_map/all_gather | solution.py:44
  32.7 2.7 copy.28
  36.1 104.4 %all-gather.9.cloned.1.call-done = bf16[1664,3,416]{2,1,0:T(4,128)(2,1)} async-done(((bf16[208,3,416]{2,1,0:T(4,128)(2,1)}), bf16[1664,3,416]{2,1,0:T(4,128)(2,1)}) %all-gather.9.cloned.1.call-update) | async-done | bytes 4153360 | tf_op jit(solution)/shard_map/all_gather | solution.py:48
  140.5 11.3 %copy.30 = bf16[1664,3,416]{0,2,1:T(8,128)(2,1)} copy(bf16[1664,3,416]{2,1,0:T(4,128)(2,1)} %all-gather.9.cloned.1.call-done) | data formatting | bytes 8306688 | tf_op jit(solution)/shard_map/all_gather | solution.py:48
  151.7 4.8 convolution_convert_fusion
  157.3 2.1 fusion.109
  160.0 26.7 %all-gather.11.cloned.1.call-done = bf16[416,1664]{0,1:T(8,128)(2,1)} async-done(((bf16[416,208]{0,1:T(8,128)(2,1)}), bf16[416,1664]{0,1:T(8,128)(2,1)}) %all-gather.11.cloned.1.call-update) | async-done | bytes 1384464 | tf_op jit(solution)/shard_map/all_gather | solution.py:60
  186.7 4.4 fusion.110
  192.5 70.4 %all-reduce.3.cloned.1.call-done = f32[512,1664]{1,0:T(8,128)} async-done(((f32[512,1664]{1,0:T(8,128)}), f32[512,1664]{1,0:T(8,128)}) %all-reduce.3.cloned.1.call-update) | async-done | bytes 3407888 | tf_op jit(solution)/shard_map/psum | solution.py:24
  262.9 2.7 convert_reduce_fusion
  265.6 105.1 %all-gather.13.cloned.1.call-done = bf16[1664,2048]{1,0:T(8,128)(2,1)} async-done(((bf16[208,2048]{1,0:T(8,128)(2,1)}), bf16[1664,2048]{1,0:T(8,128)(2,1)}) %all-gather.13.cloned.1.call-update) | async-done | bytes 6815760 | tf_op jit(solution)/shard_map/all_gather | solution.py:65
  370.6 105.8 %all-gather.15.cloned.1.call-done = bf16[2048,1664]{0,1:T(8,128)(2,1)} async-done(((bf16[2048,208]{0,1:T(8,128)(2,1)}), bf16[2048,1664]{0,1:T(8,128)(2,1)}) %all-gather.15.cloned.1.call-update) | async-done | bytes 6815760 | tf_op jit(solution)/shard_map/all_gather | solution.py:69
  476.5 21.5 %fusion.20 = f32[512,1664]{1,0:T(8,128)} fusion(bf16[2048,1664]{0,1:T(8,128)(2,1)} %all-gather.15.cloned.1.call-done, bf16[1664,2048]{1,0:T(8,128)(2,1)} %all-gather.13.cloned.1.call-done, bf16[512,1664]{1,0:T(8,128)(2,1)S(1)} %get-tuple-element.7, f32[512]{0:T(512)S(1)} %get-tuple-element.13, f32[512]{0:T(512)S(1)} %get-tuple-element.12), kind=kOutput, calls=%fused_computation.42 | convolution fusion | flops 7050887168 | bytes 18747392 | tf_op jit(solution)/shard_map/dot_general | solution.py:67
  499.2 69.8 %all-reduce.5.cloned.1.call-done = f32[512,1664]{1,0:T(8,128)} async-done(((f32[512,1664]{1,0:T(8,128)}), f32[512,1664]{1,0:T(8,128)}) %all-reduce.5.cloned.1.call-update) | async-done | bytes 3407888 | tf_op jit(solution)/shard_map/psum | solution.py:24
  569.0 2.2 fusion.18
  572.4 1.3 copy.35
  573.8 42.4 %psum.23 = f32[8]{0:T(128)S(1)} all-reduce(f32[8]{0:T(128)S(1)} %select_reduce_fusion.1), channel_id=1, replica_groups=mesh['gx'=4,'gy'=8] {'gx','gy'}, use_global_device_ids=true, to_apply=%region_11.12 | all-reduce | flops 8 | bytes 64 | tf_op jit(solution)/shard_map/psum | solution.py:87
  616.2 2.3 gather_fusion
  618.5 1.2 gather.7
  620.2 141.2 %all-gather.17.cloned.1.call-done = bf16[6656,1024]{1,0:T(8,128)(2,1)} async-done(((bf16[832,1024]{1,0:T(8,128)(2,1)}), bf16[6656,1024]{1,0:T(8,128)(2,1)}) %all-gather.17.cloned.1.call-update) | async-done | bytes 13631504 | tf_op jit(solution)/shard_map/all_gather | solution.py:85
  761.5 8.4 %fusion.108 = (f32[]{:T(128)}, bf16[128,1024]{1,0:T(8,128)(2,1)}) fusion(bf16[6656,1024]{1,0:T(8,128)(2,1)} %all-gather.17.cloned.1.call-done, pred[128,6656]{1,0:T(8,128)(4,1)} %bitcast.26, bf16[128,6656]{1,0:T(8,128)(2,1)S(1)} %gather.7), kind=kOutput, calls=%fused_computation.138 | convolution fusion | flops 1745944576 | bytes 16449540 | tf_op jit(solution)/shard_map/dot_general | solution.py:19
  769.9 38.6 %pmax.7 = f32[]{:T(128)} all-reduce(f32[]{:T(128)} %get-tuple-element.10), channel_id=1, replica_groups=mesh['gx'=4,'gy'=8] {'gx','gy'}, use_global_device_ids=true, to_apply=%region_13.14 | all-reduce | flops 1 | bytes 8 | tf_op jit(solution)/shard_map/pmax | solution.py:88
  (41 shorter events, 8.0 us)
Async XLA Ops:
  7.2 25.5 %all-gather.7.cloned.1.call-start = ((), (), s32[]{:S(2)}) async-start(), calls=%async_computation | async-start | bytes 2129920 | tf_op jit(solution)/shard_map/all_gather | solution.py:44
  7.9 132.6 %all-gather.9.cloned.1.call-start = ((), (), s32[]{:S(2)}) async-start(), calls=%async_computation.1 | async-start | bytes 7667712 | tf_op jit(solution)/shard_map/all_gather | solution.py:48
  10.6 176.1 %all-gather.11.cloned.1.call-start = ((), (), s32[]{:S(2)}) async-start(), calls=%async_computation.2 | async-start | bytes 1916928 | tf_op jit(solution)/shard_map/all_gather | solution.py:60
  12.4 250.5 %all-reduce.3.cloned.1.call-start = ((), (), s32[]{:S(2)}) async-start(), calls=%async_computation.3 | async-start | bytes 6815744 | tf_op jit(solution)/shard_map/psum | solution.py:24
  191.1 179.6 %all-gather.13.cloned.1.call-start = ((), (), s32[]{:S(2)}) async-start(), calls=%async_computation.4 | async-start | bytes 7667712 | tf_op jit(solution)/shard_map/all_gather | solution.py:65
  191.7 284.8 %all-gather.15.cloned.1.call-start = ((), (), s32[]{:S(2)}) async-start(), calls=%async_computation.5 | async-start | bytes 7667712 | tf_op jit(solution)/shard_map/all_gather | solution.py:69
  192.3 376.7 %all-reduce.5.cloned.1.call-start = ((), (), s32[]{:S(2)}) async-start(), calls=%async_computation.6 | async-start | bytes 6815744 | tf_op jit(solution)/shard_map/psum | solution.py:24
  497.9 0.8 copy-start.1
  497.9 1.2 copy-start.2
  498.0 263.5 %all-gather.17.cloned.1.call-start = ((), (), s32[]{:S(2)}) async-start(), calls=%async_computation.7 | async-start | bytes 15335424 | tf_op jit(solution)/shard_map/all_gather | solution.py:85
  498.7 72.9 %copy-start = (s32[512]{0:T(512)S(1)}, s32[512]{0:T(512)}, u32[]{:S(2)}) copy-start(s32[512]{0:T(512)} %param.10) | copy-start | bytes 6148
Sparse Core Ops, SparseCore 0:
  9.6 23.0 all-gather.6
  34.9 105.5 all-gather.8
  143.2 43.4 all-gather.10
  191.2 71.6 all-reduce.2
  264.9 105.6 all-gather.12
  372.7 103.7 all-gather.14
  498.1 70.8 all-reduce.4
  571.2 190.2 all-gather.16
where the time goes:
time: 816 us; the launch traced here: 815 us
  waiting for transfers between devices  645 us (79%)
  blocking collectives  81.1 us (10%)
  matrix products  40.3 us (5%)
  local copies, waits for them, and re-layouts  24.7 us (3%)
  between operations  14.3 us (2%)
  other arithmetic  9.36 us (1%)
    all_gather x1, waiting for transfers between devices, per_device(): lax.all_gather(merge_weight, 'gy', axis=0, tiled=True)  141 us
    psum x2, waiting for transfers between devices, finish_sum(): summed = lax.psum(head_partial, 'gx')  140 us
    all_gather x1, waiting for transfers between devices, per_device(): lax.all_gather(down_weight, 'gy', axis=1, tiled=True)  106 us
    all_gather x1, waiting for transfers between devices, per_device(): lax.all_gather(up_weight, 'gy', axis=0, tiled=True)  105 us
    all_gather x1, waiting for transfers between devices, per_device(): lax.all_gather(qkv_weight, 'gy', axis=0, tiled=True)  104 us
    psum x1, blocking collectives, per_device(): request_sq = lax.psum(request_part, ('gx', 'gy'))  42.4 us
    pmax x1, blocking collectives, per_device(): top_logit = lax.pmax(local_top, ('gx', 'gy'))  38.6 us
    all_gather x1, waiting for transfers between devices, per_device(): lax.all_gather(out_weight, 'gy', axis=1, tiled=True)  26.7 us
  transfers between devices with their start and end apart: 8, of which 8 were waited for; matrix products, arithmetic and copies ran while one was open for 5% of the time, Pallas kernels for 0%

commit v1 on v0

--- a/solution.py
+++ b/solution.py
@@ -21,7 +21,8 @@
 
 def finish_sum(head_partial, stream_full, feat_share):
     own_index = lax.axis_index("gx")
-    summed = lax.psum(head_partial, "gx")
+    terms = lax.all_gather(head_partial, "gx", axis=0, tiled=False)
+    summed = terms.sum(axis=0)
     new_full = (stream_full.astype(jnp.float32) + summed).astype(jnp.bfloat16)
     new_share = lax.dynamic_slice_in_dim(new_full, own_index * feat_share, feat_share, 1)
     return (new_full, new_share)

time: 816 us -> 888 us (1.088)
  waiting for transfers between devices: 645 us -> 701 us
  other arithmetic: 9.36 us -> 25.6 us
    all_gather x0 -> x2, waiting for transfers between devices: none -> 169 us  [finish_sum(): terms = lax.all_gather(head_partial, 'gx', axis=0, tiled=False)]
    psum x2 -> x0, waiting for transfers between devices: 140 us -> none  [finish_sum(): summed = lax.psum(head_partial, 'gx')]
    all_gather x1, waiting for transfers between devices: 141 us -> 176 us  [per_device(): lax.all_gather(merge_weight, 'gy', axis=0, tiled=True)]
    reduce_sum x0 -> x2, other arithmetic: none -> 15.7 us  [finish_sum(): summed = terms.sum(axis=0)]
  transfers between devices with their start and end apart: 8 -> 8, of which waited for: 8 -> 8; matrix products, arithmetic and copies ran while one was open for 5% -> 6% of each run, Pallas kernels for 0% -> 0%
where the time goes in v1:
time: 888 us; the launch traced here: 887 us
  waiting for transfers between devices  701 us (79%)
  blocking collectives  79.5 us (9%)
  matrix products  41.1 us (5%)
  local copies, waits for them, and re-layouts  25.6 us (3%)
  other arithmetic  25.6 us (3%)
  between operations  14.2 us (2%)
    all_gather x1, waiting for transfers between devices, per_device(): lax.all_gather(merge_weight, 'gy', axis=0, tiled=True)  176 us
    all_gather x2, waiting for transfers between devices, finish_sum(): terms = lax.all_gather(head_partial, 'gx', axis=0, tiled=False)  169 us
    all_gather x1, waiting for transfers between devices, per_device(): lax.all_gather(down_weight, 'gy', axis=1, tiled=True)  106 us
    all_gather x1, waiting for transfers between devices, per_device(): lax.all_gather(qkv_weight, 'gy', axis=0, tiled=True)  104 us
    all_gather x1, waiting for transfers between devices, per_device(): lax.all_gather(up_weight, 'gy', axis=0, tiled=True)  96.9 us
    psum x1, blocking collectives, per_device(): request_sq = lax.psum(request_part, ('gx', 'gy'))  40.9 us
    pmax x1, blocking collectives, per_device(): top_logit = lax.pmax(local_top, ('gx', 'gy'))  38.6 us
    all_gather x1, waiting for transfers between devices, per_device(): lax.all_gather(out_weight, 'gy', axis=1, tiled=True)  26.8 us
  transfers between devices with their start and end apart: 8, of which 8 were waited for; matrix products, arithmetic and copies ran while one was open for 6% of the time, Pallas kernels for 0%

profile of v1, /device:TPU:0, one launch (start us, length us, event | category | flops | bytes accessed | tf_op | source)
XLA Modules:
  0.0 887.2 jit_solution(16623817258390330057)
XLA Ops:
  7.9 2.6 copy.29
  13.4 19.3 %all-gather.11.cloned.1.call-done = bf16[512,1664]{0,1:T(8,128)(2,1)} async-done(((bf16[512,416]{0,1:T(8,128)(2,1)}), bf16[512,1664]{0,1:T(8,128)(2,1)}) %all-gather.11.cloned.1.call-update) | async-done | bytes 1703952 | tf_op jit(solution)/shard_map/all_gather | solution.py:45
  32.7 2.7 copy.28
  36.1 104.4 %all-gather.13.cloned.1.call-done = bf16[1664,3,416]{2,1,0:T(4,128)(2,1)} async-done(((bf16[208,3,416]{2,1,0:T(4,128)(2,1)}), bf16[1664,3,416]{2,1,0:T(4,128)(2,1)}) %all-gather.13.cloned.1.call-update) | async-done | bytes 4153360 | tf_op jit(solution)/shard_map/all_gather | solution.py:49
  140.5 11.3 %copy.30 = bf16[1664,3,416]{0,2,1:T(8,128)(2,1)} copy(bf16[1664,3,416]{2,1,0:T(4,128)(2,1)} %all-gather.13.cloned.1.call-done) | data formatting | bytes 8306688 | tf_op jit(solution)/shard_map/all_gather | solution.py:49
  151.7 4.8 convolution_convert_fusion
  157.3 2.1 fusion.109
  159.9 26.8 %all-gather.15.cloned.1.call-done = bf16[416,1664]{0,1:T(8,128)(2,1)} async-done(((bf16[416,208]{0,1:T(8,128)(2,1)}), bf16[416,1664]{0,1:T(8,128)(2,1)}) %all-gather.15.cloned.1.call-update) | async-done | bytes 1384464 | tf_op jit(solution)/shard_map/all_gather | solution.py:61
  186.7 4.5 fusion.110
  192.7 85.8 %all-gather.23.cloned.1.call-done = f32[2048,1664]{1,0:T(8,128)} async-done(((f32[512,1664]{1,0:T(8,128)}), f32[2048,1664]{1,0:T(8,128)}) %all-gather.23.cloned.1.call-update) | async-done | bytes 13631504 | tf_op jit(solution)/shard_map/all_gather | solution.py:24
  278.4 7.8 reduce_sum.93
  286.3 2.9 convert_reduce_fusion
  289.2 96.9 %all-gather.17.cloned.1.call-done = bf16[1664,2048]{1,0:T(8,128)(2,1)} async-done(((bf16[208,2048]{1,0:T(8,128)(2,1)}), bf16[1664,2048]{1,0:T(8,128)(2,1)}) %all-gather.17.cloned.1.call-update) | async-done | bytes 6815760 | tf_op jit(solution)/shard_map/all_gather | solution.py:66
  386.1 105.8 %all-gather.19.cloned.1.call-done = bf16[2048,1664]{0,1:T(8,128)(2,1)} async-done(((bf16[2048,208]{0,1:T(8,128)(2,1)}), bf16[2048,1664]{0,1:T(8,128)(2,1)}) %all-gather.19.cloned.1.call-update) | async-done | bytes 6815760 | tf_op jit(solution)/shard_map/all_gather | solution.py:70
  491.9 21.6 %fusion.20 = f32[512,1664]{1,0:T(8,128)} fusion(bf16[2048,1664]{0,1:T(8,128)(2,1)} %all-gather.19.cloned.1.call-done, bf16[1664,2048]{1,0:T(8,128)(2,1)} %all-gather.17.cloned.1.call-done, bf16[512,1664]{1,0:T(8,128)(2,1)S(1)} %get-tuple-element.7, f32[512]{0:T(512)S(1)} %get-tuple-element.13, f32[512]{0:T(512)S(1)} %get-tuple-element.12), kind=kOutput, calls=%fused_computation.42 | convolution fusion | flops 7050887168 | bytes 18747392 | tf_op jit(solution)/shard_map/dot_general | solution.py:68
  516.6 83.4 %all-gather.25.cloned.1.call-done = f32[2048,1664]{1,0:T(8,128)} async-done(((f32[512,1664]{1,0:T(8,128)}), f32[2048,1664]{1,0:T(8,128)}) %all-gather.25.cloned.1.call-update) | async-done | bytes 13631504 | tf_op jit(solution)/shard_map/all_gather | solution.py:24
  600.0 7.8 reduce_sum.96
  607.8 2.6 fusion.18
  610.4 2.3 gather_fusion
  612.7 2.1 gather.7
  615.5 175.9 %all-gather.21.cloned.1.call-done = bf16[6656,1024]{1,0:T(8,128)(2,1)} async-done(((bf16[832,1024]{1,0:T(8,128)(2,1)}), bf16[6656,1024]{1,0:T(8,128)(2,1)}) %all-gather.21.cloned.1.call-update) | async-done | bytes 13631504 | tf_op jit(solution)/shard_map/all_gather | solution.py:86
  791.4 8.9 %fusion.108 = (f32[]{:T(128)}, bf16[128,1024]{1,0:T(8,128)(2,1)}) fusion(bf16[6656,1024]{1,0:T(8,128)(2,1)} %all-gather.21.cloned.1.call-done, pred[128,6656]{1,0:T(8,128)(4,1)} %bitcast.30, bf16[128,6656]{1,0:T(8,128)(2,1)} %gather.7), kind=kOutput, calls=%fused_computation.138 | convolution fusion | flops 1745944576 | bytes 16449540 | tf_op jit(solution)/shard_map/dot_general | solution.py:19
  800.3 38.6 %pmax.7 = f32[]{:T(128)} all-reduce(f32[]{:T(128)} %get-tuple-element.10), channel_id=1, replica_groups=mesh['gx'=4,'gy'=8] {'gx','gy'}, use_global_device_ids=true, to_apply=%region_13.14 | all-reduce | flops 1 | bytes 8 | tf_op jit(solution)/shard_map/pmax | solution.py:89
  838.9 40.9 %psum.7 = f32[8]{0:T(128)S(1)} all-reduce(f32[8]{0:T(128)S(1)} %select_reduce_fusion.1), channel_id=1, replica_groups=mesh['gx'=4,'gy'=8] {'gx','gy'}, use_global_device_ids=true, to_apply=%region_11.12 | all-reduce | flops 8 | bytes 64 | tf_op jit(solution)/shard_map/psum | solution.py:88
  (43 shorter events, 11.0 us)
Async XLA Ops:
  7.2 25.5 %all-gather.11.cloned.1.call-start = ((), (), s32[]{:S(2)}) async-start(), calls=%async_computation | async-start | bytes 2129920 | tf_op jit(solution)/shard_map/all_gather | solution.py:45
  7.9 132.6 %all-gather.13.cloned.1.call-start = ((), (), s32[]{:S(2)}) async-start(), calls=%async_computation.1 | async-start | bytes 7667712 | tf_op jit(solution)/shard_map/all_gather | solution.py:49
  10.6 176.1 %all-gather.15.cloned.1.call-start = ((), (), s32[]{:S(2)}) async-start(), calls=%async_computation.2 | async-start | bytes 1916928 | tf_op jit(solution)/shard_map/all_gather | solution.py:61
  12.4 266.0 %all-gather.23.cloned.1.call-start = ((), (), s32[]{:S(2)}) async-start(), calls=%async_computation.6 | async-start | bytes 17039360 | tf_op jit(solution)/shard_map/all_gather | solution.py:24
  191.3 194.8 %all-gather.17.cloned.1.call-start = ((), (), s32[]{:S(2)}) async-start(), calls=%async_computation.3 | async-start | bytes 7667712 | tf_op jit(solution)/shard_map/all_gather | solution.py:66
  191.9 300.0 %all-gather.19.cloned.1.call-start = ((), (), s32[]{:S(2)}) async-start(), calls=%async_computation.4 | async-start | bytes 7667712 | tf_op jit(solution)/shard_map/all_gather | solution.py:70
  192.4 407.5 %all-gather.25.cloned.1.call-start = ((), (), s32[]{:S(2)}) async-start(), calls=%async_computation.7 | async-start | bytes 17039360 | tf_op jit(solution)/shard_map/all_gather | solution.py:24
  513.5 0.8 copy-start.1
  513.5 3.0 copy-start.2
  513.5 277.9 %all-gather.21.cloned.1.call-start = ((), (), s32[]{:S(2)}) async-start(), calls=%async_computation.5 | async-start | bytes 15335424 | tf_op jit(solution)/shard_map/all_gather | solution.py:86
  610.4 4.8 copy-start
Sparse Core Ops, SparseCore 0:
  9.6 23.0 all-gather.10
  34.9 105.5 all-gather.12
  143.2 43.4 all-gather.14
  191.4 86.9 all-gather.22
  280.5 105.5 all-gather.16
  388.1 103.7 all-gather.18
  513.7 86.2 all-gather.24
  602.2 189.2 all-gather.20
